TPU v7x, 32 devices: a whole 2x2x4 slice. The times are simulated.
32 devices in a mesh: tensor: 4 (over z), context: 4 (over y, core), dp: 2 (over x).
Axes of the slice: x: 2, y: 2, z: 4, core: 2. Of those that a mesh axis runs over, the one named last changes fastest.
Arguments:
- inputs: bfloat16 [2, 3072, 768], P('dp', ('context', 'tensor')), may hold values from -6 to 6
- first_gain: float32 [768], replicated, may hold values from 0.5 to 1.5
- first_shift: float32 [768], replicated, may hold values from -1 to 1
- project_weight: bfloat16 [3, 768, 768], P(None, None, 'tensor'), may hold values from -0.21875 to 0.21875
- project_bias: float32 [2, 768], P(None, 'tensor'), may hold values from -1.5 to 1.5
- attend_weight: bfloat16 [768, 768], P('tensor'), may hold values from -1.25 to 1.25
- attend_bias: float32 [768], replicated, may hold values from -1.5 to 1.5
- second_gain: float32 [768], replicated, may hold values from 0.5 to 1.5
- second_shift: float32 [768], replicated, may hold values from -1 to 1
- expand_weight: bfloat16 [768, 3072], P(None, 'tensor'), may hold values from -0.21875 to 0.21875
- expand_bias: float32 [3072], P('tensor'), may hold values from -1.5 to 1.5
- shrink_weight: bfloat16 [3072, 768], P('tensor'), may hold values from -0.109375 to 0.109375
- shrink_bias: float32 [768], replicated, may hold values from -1.5 to 1.5
- segments: int32 [2, 3072], P('dp'), may hold values from 0 to 15, never falling along the last dimension, each value on 1 to 1536 neighbouring positions
- block_order: int32 [8], replicated, may hold values from 0 to 7, each once
- cotangent: bfloat16 [2, 3072, 768], P('dp', ('context', 'tensor')), may hold values from -6 to 6
Outputs:
- outputs: bfloat16 [2, 3072, 768], P('dp', ('context', 'tensor'))
- grad_inputs: bfloat16 [2, 3072, 768], P('dp', ('context', 'tensor'))
- grad_first_gain: float32 [768], replicated
- grad_first_shift: float32 [768], replicated
- grad_project_weight: float32 [3, 768, 768], P(None, None, 'tensor')
- grad_project_bias: float32 [2, 768], P(None, 'tensor')
- grad_attend_weight: float32 [768, 768], P('tensor')
- grad_attend_bias: float32 [768], replicated
- grad_second_gain: float32 [768], replicated
- grad_second_shift: float32 [768], replicated
- grad_expand_weight: float32 [768, 3072], P(None, 'tensor')
- grad_expand_bias: float32 [3072], P('tensor')
- grad_shrink_weight: float32 [3072, 768], P('tensor')
- grad_shrink_bias: float32 [768], replicated
Inputs may be any that keep to these rules, and one draw needn't show every extreme that they name: `segments`: in each sequence the document numbers never fall; every number appears, each document has 1 to 1536 tokens and one has exactly 1536. Each value appears once: stored block b of 384 tokens holds natural block block_order[b].
All inputs are finite; a program needn't handle non-finite values.
Results may differ from a plain program's by a relative error of at most 0.02.
Values may be sent and summed in bfloat16 or wider, within the bound.
A program may use at most 128 MiB of HBM per device.

v0:
```python
import jax
import jax.numpy as jnp
from jax import lax
from jax.sharding import PartitionSpec as P

HEAD_DIM = 64
NEG_FILL = -1e30
NORM_EPS = 1e-05


def layer_norm(values):
    centre = jnp.mean(values, axis=-1, keepdims=True)
    shifted = values - centre
    spread = jnp.mean(shifted * shifted, axis=-1, keepdims=True)
    return shifted * lax.rsqrt(spread + NORM_EPS)


def affine_norm(values, gain, shift):
    return layer_norm(values) * gain + shift


def gelu_tanh(values):
    return jax.nn.gelu(values, approximate=True)


def stored_places(order, half_rows, seq_len):
    index = jnp.arange(seq_len, dtype=jnp.int32)
    slots = jnp.arange(order.shape[0], dtype=jnp.int32)
    chosen = jnp.sum(
        jnp.where((index // half_rows)[:, None] == slots[None, :], order[None, :], 0), axis=1
    )
    return chosen * half_rows + index % half_rows


def allowed_pairs(query_place, query_seg, key_place, key_seg):
    return (query_seg[:, None] == key_seg[None, :]) & (key_place[None, :] <= query_place[:, None])


def split_heads(values):
    return values.reshape(values.shape[0], -1, HEAD_DIM)


def cross_rows(left, right):
    return lax.dot_general(
        left, right, (((0,), (0,)), ((), ())), preferred_element_type=jnp.float32
    )


def over_blocks(step_fn, running, arrays, size):
    total_rows = arrays[0].shape[0]
    blocks = total_rows // size
    stacked = tuple((item.reshape((blocks, size) + item.shape[1:]) for item in arrays))
    starts = jnp.arange(blocks, dtype=jnp.int32) * size

    def inner(state, element):
        return (step_fn(state, element[0], element[1]), None)

    running, _ = lax.scan(inner, running, (stacked, starts))
    return running


def per_device(
    inputs,
    first_gain,
    first_shift,
    project_weight,
    project_bias,
    attend_weight,
    attend_bias,
    second_gain,
    second_shift,
    expand_weight,
    expand_bias,
    shrink_weight,
    shrink_bias,
    segments,
    block_order,
    cotangent,
):
    own_rows = inputs.shape[1]
    local_width = project_weight.shape[2]
    head_count = local_width // HEAD_DIM
    block_rows = own_rows * lax.axis_size("tensor")
    seq_len = block_rows * lax.axis_size("context")
    half_rows = block_rows // 2
    score_scale = HEAD_DIM ** (-0.5)
    places = stored_places(block_order, half_rows, seq_len)
    seg_stored = jnp.take(segments[0], places)
    my_first = lax.axis_index("context") * block_rows
    query_place = lax.dynamic_slice_in_dim(places, my_first, block_rows)
    query_seg = lax.dynamic_slice_in_dim(seg_stored, my_first, block_rows)
    tokens_own = inputs[0].astype(jnp.float32)
    hidden1 = affine_norm(tokens_own, first_gain, first_shift).astype(jnp.bfloat16)
    hidden1_full = lax.all_gather(hidden1, "tensor", axis=0, tiled=True)
    projected = jnp.einsum(
        "rd,kde->kre", hidden1_full, project_weight, preferred_element_type=jnp.float32
    )
    query_rows = (projected[0] + project_bias[0]).astype(jnp.bfloat16)
    key_rows = projected[1].astype(jnp.bfloat16)
    value_rows = (projected[2] + project_bias[1]).astype(jnp.bfloat16)
    query_heads = split_heads(query_rows)

    def key_mask(key_first, amount):
        key_place = lax.dynamic_slice_in_dim(places, key_first, amount)
        key_seg = lax.dynamic_slice_in_dim(seg_stored, key_first, amount)
        return allowed_pairs(query_place, query_seg, key_place, key_seg)[:, None, :]

    def forward_step(running, pieces, key_first):
        row_max, row_sum, weighted = running
        key_heads = split_heads(pieces[0])
        allowed = key_mask(key_first, pieces[0].shape[0])
        scores = (
            jnp.einsum("qhe,khe->qhk", query_heads, key_heads, preferred_element_type=jnp.float32)
            * score_scale
        )
        scores = jnp.where(allowed, scores, NEG_FILL)
        new_max = jnp.maximum(row_max, jnp.max(scores, axis=-1))
        factor = jnp.exp(row_max - new_max)
        weights = jnp.where(allowed, jnp.exp(scores - new_max[..., None]), 0.0)
        row_sum = row_sum * factor + jnp.sum(weights, axis=-1)
        weighted = weighted * factor[..., None] + jnp.einsum(
            "qhk,khe->qhe",
            weights.astype(jnp.bfloat16),
            split_heads(pieces[1]),
            preferred_element_type=jnp.float32,
        )
        return (new_max, row_sum, weighted)

    start_state = (
        jnp.full((block_rows, head_count), NEG_FILL, jnp.float32),
        jnp.zeros((block_rows, head_count), jnp.float32),
        jnp.zeros((block_rows, head_count, HEAD_DIM), jnp.float32),
    )
    row_max, row_sum, weighted = over_blocks(
        forward_step,
        start_state,
        (
            lax.all_gather(key_rows, "context", axis=0, tiled=True),
            lax.all_gather(value_rows, "context", axis=0, tiled=True),
        ),
        block_rows,
    )
    log_total = row_max + jnp.log(row_sum)
    attended = weighted / row_sum[..., None]
    attended_low = attended.reshape(block_rows, local_width).astype(jnp.bfloat16)
    part = attended_low
    branch = lax.psum_scatter(
        jnp.dot(part, attend_weight, preferred_element_type=jnp.float32).astype(jnp.bfloat16),
        "tensor",
        scatter_dimension=0,
        tiled=True,
    ).astype(jnp.float32)
    middle = tokens_own + branch + attend_bias
    hidden2 = affine_norm(middle, second_gain, second_shift).astype(jnp.bfloat16)
    hidden2_full = lax.all_gather(hidden2, "tensor", axis=0, tiled=True)
    pre_act = jnp.dot(hidden2_full, expand_weight, preferred_element_type=jnp.float32) + expand_bias
    activ = gelu_tanh(pre_act).astype(jnp.bfloat16)
    part = activ
    feed_sum = lax.psum_scatter(
        jnp.dot(part, shrink_weight, preferred_element_type=jnp.float32).astype(jnp.bfloat16),
        "tensor",
        scatter_dimension=0,
        tiled=True,
    ).astype(jnp.float32)
    outputs = (middle + feed_sum + shrink_bias).astype(jnp.bfloat16)[None]
    grad_out = cotangent[0]
    grad_full = lax.all_gather(grad_out, "tensor", axis=0, tiled=True)
    grad_shrink = cross_rows(activ, grad_full)
    grad_shrink_bias = jnp.sum(grad_out.astype(jnp.float32), axis=0)
    grad_act = jnp.dot(grad_full, shrink_weight.T, preferred_element_type=jnp.float32)
    grad_pre = jax.vjp(gelu_tanh, pre_act)[1](grad_act)[0].astype(jnp.bfloat16)
    grad_expand = cross_rows(hidden2_full, grad_pre)
    grad_expand_bias = jnp.sum(grad_pre.astype(jnp.float32), axis=0)
    part = grad_pre
    grad_hidden2 = lax.psum_scatter(
        jnp.dot(part, expand_weight.T, preferred_element_type=jnp.float32).astype(jnp.bfloat16),
        "tensor",
        scatter_dimension=0,
        tiled=True,
    ).astype(jnp.float32)
    second_pull = jax.vjp(affine_norm, middle, second_gain, second_shift)[1]
    grad_middle_norm, grad_second_gain, grad_second_shift = second_pull(grad_hidden2)
    grad_middle = grad_out.astype(jnp.float32) + grad_middle_norm
    grad_middle_low = grad_middle.astype(jnp.bfloat16)
    grad_middle_full = lax.all_gather(grad_middle_low, "tensor", axis=0, tiled=True)
    grad_attend = cross_rows(attended_low, grad_middle_full)
    grad_attend_bias = jnp.sum(grad_middle_low.astype(jnp.float32), axis=0)
    grad_attended = jnp.dot(
        grad_middle_full, attend_weight.T, preferred_element_type=jnp.float32
    ).astype(jnp.bfloat16)
    grad_heads = split_heads(grad_attended)
    delta = jnp.sum(grad_heads.astype(jnp.float32) * attended, axis=-1)

    def probs_for(q_heads, k_heads, lse_rows, allowed):
        scores = (
            jnp.einsum("qhe,khe->qhk", q_heads, k_heads, preferred_element_type=jnp.float32)
            * score_scale
        )
        return jnp.where(allowed, jnp.exp(scores - lse_rows[..., None]), 0.0)

    def grad_scores(weights, out_heads, v_heads, delta_rows):
        grad_weights = jnp.einsum(
            "qhe,khe->qhk", out_heads, v_heads, preferred_element_type=jnp.float32
        )
        return (weights * (grad_weights - delta_rows[..., None])).astype(jnp.bfloat16)

    zero_rows = jnp.zeros((block_rows, head_count, HEAD_DIM), jnp.float32)
    key_all, value_all = (
        lax.all_gather(key_rows, "context", axis=0, tiled=True),
        lax.all_gather(value_rows, "context", axis=0, tiled=True),
    )

    def key_pass(running, key_first):
        key_heads = split_heads(lax.dynamic_slice_in_dim(key_all, key_first, block_rows))
        value_heads = split_heads(lax.dynamic_slice_in_dim(value_all, key_first, block_rows))
        weights = probs_for(query_heads, key_heads, log_total, key_mask(key_first, block_rows))
        score_grad = grad_scores(weights, grad_heads, value_heads, delta)
        running = (
            running
            + jnp.einsum("qhk,khe->qhe", score_grad, key_heads, preferred_element_type=jnp.float32)
            * score_scale
        )
        grad_key = (
            jnp.einsum("qhk,qhe->khe", score_grad, query_heads, preferred_element_type=jnp.float32)
            * score_scale
        )
        grad_value = jnp.einsum(
            "qhk,qhe->khe",
            weights.astype(jnp.bfloat16),
            grad_heads,
            preferred_element_type=jnp.float32,
        )
        return (
            running,
            jnp.concatenate(
                [
                    grad_key.reshape(block_rows, local_width),
                    grad_value.reshape(block_rows, local_width),
                ],
                axis=1,
            ),
        )

    key_starts = jnp.arange(seq_len // block_rows, dtype=jnp.int32) * block_rows
    grad_query, key_terms = lax.scan(key_pass, zero_rows, key_starts)
    key_value_grads = lax.psum_scatter(
        key_terms.reshape(seq_len, 2 * local_width).astype(jnp.bfloat16),
        "context",
        scatter_dimension=0,
        tiled=True,
    ).astype(jnp.float32)
    grad_key = key_value_grads[:, :local_width]
    grad_value = key_value_grads[:, local_width:]
    grad_project_rows = jnp.stack(
        [grad_query.reshape(block_rows, local_width), grad_key, grad_value]
    ).astype(jnp.bfloat16)
    grad_project = jnp.einsum(
        "rd,kre->kde", hidden1_full, grad_project_rows, preferred_element_type=jnp.float32
    )
    grad_project_bias = jnp.stack(
        [
            jnp.sum(grad_project_rows[0].astype(jnp.float32), axis=0),
            jnp.sum(grad_project_rows[2].astype(jnp.float32), axis=0),
        ]
    )
    part = grad_project_rows
    grad_hidden1 = lax.psum_scatter(
        jnp.einsum("kre,kde->rd", part, project_weight, preferred_element_type=jnp.float32).astype(
            jnp.bfloat16
        ),
        "tensor",
        scatter_dimension=0,
        tiled=True,
    ).astype(jnp.float32)
    first_pull = jax.vjp(affine_norm, tokens_own, first_gain, first_shift)[1]
    grad_tokens_norm, grad_first_gain, grad_first_shift = first_pull(grad_hidden1)
    grad_inputs = (grad_middle + grad_tokens_norm).astype(jnp.bfloat16)[None]
    summed = lax.psum(
        (grad_project, grad_project_bias, grad_attend, grad_expand, grad_expand_bias, grad_shrink),
        ("context", "dp"),
    )
    vectors = lax.psum(
        (
            grad_first_gain,
            grad_first_shift,
            grad_attend_bias,
            grad_second_gain,
            grad_second_shift,
            grad_shrink_bias,
        ),
        ("tensor", "context", "dp"),
    )
    return (
        outputs,
        grad_inputs,
        vectors[0],
        vectors[1],
        summed[0],
        summed[1],
        summed[2],
        vectors[2],
        vectors[3],
        vectors[4],
        summed[3],
        summed[4],
        summed[5],
        vectors[5],
    )


def solution(mesh):
    in_specs = (
        P("dp", ("context", "tensor"), None),
        P(),
        P(),
        P(None, None, "tensor"),
        P(None, "tensor"),
        P("tensor", None),
        P(),
        P(),
        P(),
        P(None, "tensor"),
        P("tensor"),
        P("tensor", None),
        P(),
        P("dp", None),
        P(),
        P("dp", ("context", "tensor"), None),
    )
    out_specs = (
        P("dp", ("context", "tensor"), None),
        P("dp", ("context", "tensor"), None),
        P(),
        P(),
        P(None, None, "tensor"),
        P(None, "tensor"),
        P("tensor", None),
        P(),
        P(),
        P(),
        P(None, "tensor"),
        P("tensor"),
        P("tensor", None),
        P(),
    )
    return jax.shard_map(
        per_device, mesh=mesh, in_specs=in_specs, out_specs=out_specs, check_vma=False
    )
```

profile of v0, /device:TPU:0, one launch (start us, length us, event | category | flops | bytes accessed | tf_op | source)
XLA Modules:
  0.0 606.1 jit_solution(4479381773742738639)
XLA Ops:
  10.8 1.9 fusion.54
  12.8 33.1 %all-gather.9.cloned.1.call-done = bf16[768,768]{1,0:T(8,128)(2,1)} async-done(((bf16[192,768]{1,0:T(8,128)(2,1)}), bf16[768,768]{1,0:T(8,128)(2,1)}) %all-gather.9.cloned.1.call-update) | async-done | bytes 1179664 | tf_op jit(solution)/shard_map/all_gather | solution.py:94
  45.9 2.4 fusion.88
  50.5 1.9 fusion.63
  52.7 17.4 %gather_fusion = s32[3072]{0:T(1024)S(1)} fusion(s32[3072]{0:T(1024)S(1)} %bitcast.270, s32[3072]{0:T(1024)S(1)} %broadcast_clamp_fusion), kind=kCustom, calls=%fused_computation | custom fusion | bytes 36864 | tf_op jit(solution)/shard_map/jit(_take)/gather | solution.py:88
  74.6 3.5 reshape.298
  79.5 7.2 %all-gather.11.cloned.1.call-done = bf16[3072,192]{0,1:T(8,128)(2,1)} async-done(((bf16[768,192]{0,1:T(8,128)(2,1)}), bf16[3072,192]{0,1:T(8,128)(2,1)}) %all-gather.11.cloned.1.call-update) | async-done | bytes 1179664 | tf_op jit(solution)/shard_map/all_gather | solution.py:139
  86.7 2.4 copy.58
  89.1 54.7 %while.28 = (s32[]{:T(128)}, f32[768,3]{0,1:T(4,128)S(1)}, f32[768,3]{0,1:T(4,128)}, f32[768,3,64]{0,2,1:T(8,128)S(1)}, s32[768]{0:T(1024)}, /*index=5*/s32[4]{0...) while((s32[]{:T(128)}, f32[768,3]{0,1:T(4,128)S(1)}, ...), condition=%wide.region_6.7_spmd.clone, body=%wide.region_3.6_spmd.clone.sunk | while | flops 478211328 | bytes 27009240 | solution.py:58
  97.5 1.8 fusion.149
  99.9 2.3 fusion.151
  110.7 1.8 fusion.149
  113.8 2.3 fusion.151
  124.6 1.8 fusion.149
  127.7 2.3 fusion.151
  141.5 2.3 fusion.151
  144.6 2.5 convolution_convert_fusion.2
  147.2 29.4 %reduce-scatter.6.cloned.1.call-done = bf16[192,768]{1,0:T(8,128)(2,1)} async-done(((bf16[768,768]{1,0:T(8,128)(2,1)}), bf16[192,768]{1,0:T(8,128)(2,1)}) %reduce-scatter.6.cloned.1.call-update) | async-done | bytes 294928 | tf_op jit(solution)/shard_map/reduce_scatter | solution.py:147
  179.0 1.9 add_convert_fusion.2
  181.8 28.2 %all-gather.13.cloned.1.call-done = bf16[768,768]{1,0:T(8,128)(2,1)} async-done(((bf16[192,768]{1,0:T(8,128)(2,1)}), bf16[768,768]{1,0:T(8,128)(2,1)}) %all-gather.13.cloned.1.call-update) | async-done | bytes 1179664 | tf_op jit(solution)/shard_map/all_gather | solution.py:155
  209.9 4.1 fusion.89
  214.1 26.8 %all-gather.19.cloned.1.call-done = bf16[1,768,768]{2,1,0:T(8,128)(2,1)} async-done(((bf16[1,192,768]{2,1,0:T(8,128)(2,1)}), bf16[1,768,768]{2,1,0:T(8,128)(2,1)}) %all-gather.19.cloned.1.call-update) | async-done | bytes 1179664 | tf_op jit(solution)/shard_map/all_gather | solution.py:167
  240.9 5.0 convert_reduce_fusion
  246.9 2.1 convolution_convert_fusion
  249.2 4.3 convolution_convert_fusion.1
  253.6 24.3 %reduce-scatter.10.cloned.1.call-done = bf16[192,768]{1,0:T(8,128)(2,1)} async-done(((bf16[768,768]{1,0:T(8,128)(2,1)}), bf16[192,768]{1,0:T(8,128)(2,1)}) %reduce-scatter.10.cloned.1.call-update) | async-done | bytes 294928 | tf_op jit(solution)/shard_map/reduce_scatter | solution.py:175
  277.8 1.9 fusion.60
  280.4 28.2 %reduce-scatter.8.cloned.1.call-done = bf16[192,768]{1,0:T(8,128)(2,1)} async-done(((bf16[768,768]{1,0:T(8,128)(2,1)}), bf16[192,768]{1,0:T(8,128)(2,1)}) %reduce-scatter.8.cloned.1.call-update) | async-done | bytes 294928 | tf_op jit(solution)/shard_map/reduce_scatter | solution.py:159
  308.7 2.2 fusion.85
  313.9 27.4 %all-gather.15.cloned.1.call-done = bf16[768,768]{1,0:T(8,128)(2,1)} async-done(((bf16[192,768]{1,0:T(8,128)(2,1)}), bf16[768,768]{1,0:T(8,128)(2,1)}) %all-gather.15.cloned.1.call-update) | async-done | bytes 1179664 | tf_op jit(solution)/shard_map/all_gather | solution.py:185
  341.4 1.8 convolution_convert_fusion.3
  344.0 62.4 %while.29 = (s32[]{:T(128)}, f32[768,3,64]{0,2,1:T(8,128)S(1)}, bf16[4,768,384]{1,2,0:T(8,128)(2,1)}, s32[4]{0:T(128)}, bf16[3072,192]{0,1:T(8,128)(2,1)}, /*ind...) while((s32[]{:T(128)}, f32[768,3,64]{0,2,1:T(8,128)S(1)}, ...), condition=%wide.region_16.17_spmd.clone, body=%wide.region_15.16_spmd.clone.sunk | while | flops 1153843200 | bytes 39902472 | solution.py:245
  354.1 2.7 fusion.163
  369.7 2.7 fusion.163
  385.3 2.7 fusion.163
  400.9 2.7 fusion.163
  406.4 3.4 copy.56
  409.9 32.1 %reduce-scatter.12.cloned.1.call-done = bf16[768,384]{0,1:T(8,128)(2,1)} async-done(((bf16[3072,384]{0,1:T(8,128)(2,1)}), bf16[768,384]{0,1:T(8,128)(2,1)}) %reduce-scatter.12.cloned.1.call-update) | async-done | bytes 589840 | tf_op jit(solution)/shard_map/reduce_scatter | solution.py:246
  443.1 2.3 bitcast_convert_fusion
  445.5 4.3 fusion.91
  449.8 2.8 fusion.37
  453.9 2.1 convolution_bitcast_fusion
  457.2 14.7 %all-reduce.1 = (f32[2,192]{1,0:T(2,128)}, f32[768]{0:T(1024)}) all-reduce(f32[2,192]{1,0:T(2,128)S(1)} %pad_maximum_fusion.3, f32[768]{0:T(1024)S(1)} %copy-done.32), channel_id=1, replica_groups=mesh['tensor'=4,'context'=4,'dp'=2] {'context','dp'}, use_global_device_ids=true, to_apply=%region_28.29 | all-reduce | flops 1152 | bytes 9216 | tf_op jit(solution)/shard_map/psum | solution.py:278
  471.9 3.0 reduce-scatter.14.cloned.1.call-done
  477.5 40.2 %all-reduce = (f32[768]{0:T(1024)}, f32[768]{0:T(1024)}, f32[768]{0:T(1024)}, f32[768]{0:T(1024)}, f32[768]{0:T(1024)}, /*index=5*/f32[768]{0:T(1024)}) all-reduce(f32[768]{0:T(1024)S(1)} %get-tuple-element.278, f32[768]{0:T(1024)S(1)} %get-tuple-element.281, ...), channel_id=1, replica_groups=mesh['tensor'=4,'context'=4,'dp'=2] {'tensor','context','dp'}, use_global_device_ids=true, to_apply=%region_22.23 | all-reduce | flops 4608 | bytes 36864 | tf_op jit(solution)/shard_map/psum | solution.py:282
  517.7 2.0 fusion.69
  519.7 71.8 %all-reduce.5.cloned.1.call-done = (f32[3,768,192]{1,2,0:T(8,128)}, f32[192,768]{1,0:T(8,128)}, f32[768,768]{1,0:T(8,128)}, f32[768,768]{1,0:T(8,128)}) async-done(((f32[3,768,192]{1,2,0:T(8,128)}, f32[192,768]{1,0:T(8,128)}, f32[768,768]{1,0:T(8,128)}, f32[768,768]{1,0:T(8,128)}), (f32[3,768,192]{1,2,0:T(8,128)}, f32[192,768]{1,0:T(8,128)}, f32[768,768]{1,0:T(8,128)}, ...) | async-done | bytes 7077904 | tf_op jit(solution)/shard_map/psum | solution.py:278
  591.5 2.9 copy.85
  (242 shorter events, 108.5 us)
Async XLA Ops:
  7.2 233.7 %copy-start = (bf16[768,768]{1,0:T(8,128)(2,1)S(1)}, bf16[768,768]{1,0:T(8,128)(2,1)}, u32[]{:S(2)}) copy-start(bf16[768,768]{1,0:T(8,128)(2,1)} %param.31) | copy-start | bytes 3538948
  7.2 38.7 %all-gather.9.cloned.1.call-start = ((), (), s32[]{:S(2)}) async-start(), calls=%async_computation.5 | async-start | bytes 1474560 | tf_op jit(solution)/shard_map/all_gather | solution.py:94
  8.4 1.8 copy-start.16
  12.7 61.9 %all-gather.17.cloned.1.call-start = ((), (), s32[]{:S(2)}) async-start(), calls=%async_computation.14 | async-start | bytes 1474560 | tf_op jit(solution)/shard_map/all_gather | solution.py:138
  45.9 4.5 copy-start.33
  45.9 6.6 %copy-start.34 = (s32[8]{0:T(128)S(1)}, s32[8]{0:T(128)}, u32[]{:S(2)}) copy-start(s32[8]{0:T(128)} %param.34) | copy-start | bytes 100
  48.3 4.3 copy-start.2
  50.3 36.4 %all-gather.11.cloned.1.call-start = ((), (), s32[]{:S(2)}) async-start(), calls=%async_computation.6 | async-start | bytes 1474560 | tf_op jit(solution)/shard_map/all_gather | solution.py:139
  52.4 124.3 %reduce-scatter.6.cloned.1.call-start = ((), (), s32[]{:S(2)}) async-start(), calls=%async_computation.7 | async-start | bytes 1474560 | tf_op jit(solution)/shard_map/reduce_scatter | solution.py:147
  143.8 32.8 %copy-start.3 = (bf16[1,192,768]{2,1,0:T(8,128)(2,1)S(1)}, bf16[1,192,768]{2,1,0:T(8,128)(2,1)}, u32[]{:S(2)}) copy-start(bf16[1,192,768]{2,1,0:T(8,128)(2,1)} %param.20) | copy-start | bytes 884740
  143.8 32.8 %copy-start.13 = (f32[768]{0:T(1024)S(1)}, f32[768]{0:T(1024)}, u32[]{:S(2)}) copy-start(f32[768]{0:T(1024)} %param.26) | copy-start | bytes 9220
  143.8 35.2 %copy-start.15 = (f32[768]{0:T(1024)S(1)}, f32[768]{0:T(1024)}, u32[]{:S(2)}) copy-start(f32[768]{0:T(1024)} %param.27) | copy-start | bytes 9220
  143.8 35.2 %copy-start.31 = (f32[768]{0:T(1024)S(1)}, f32[768]{0:T(1024)}, u32[]{:S(2)}) copy-start(f32[768]{0:T(1024)} %param.28) | copy-start | bytes 9220
  147.2 62.8 %all-gather.13.cloned.1.call-start = ((), (), s32[]{:S(2)}) async-start(), calls=%async_computation.8 | async-start | bytes 1474560 | tf_op jit(solution)/shard_map/all_gather | solution.py:155
  177.8 36.2 %copy-start.18 = (f32[192]{0:T(256)}, f32[192]{0:T(256)S(1)}, u32[]{:S(2)}) copy-start(f32[192]{0:T(256)S(1)} %broadcast_multiply_fusion.1) | copy-start | bytes 2308
  179.0 35.1 %copy-start.28 = (f32[192]{0:T(256)}, f32[192]{0:T(256)S(1)}, u32[]{:S(2)}) copy-start(f32[192]{0:T(256)S(1)} %multiply_reduce_fusion.1) | copy-start | bytes 2308
  179.0 35.0 %copy-start.24 = (f32[192]{0:T(256)}, f32[192]{0:T(256)S(1)}, u32[]{:S(2)}) copy-start(f32[192]{0:T(256)S(1)} %fusion.81) | copy-start | bytes 2308
  180.9 59.9 %all-gather.19.cloned.1.call-start = ((), (), s32[]{:S(2)}) async-start(), calls=%async_computation.15 | async-start | bytes 1474560 | tf_op jit(solution)/shard_map/all_gather | solution.py:167
  181.5 59.4 %copy-start.39 = (f32[768]{0:T(1024)S(1)}, f32[768]{0:T(1024)}, u32[]{:S(2)}) copy-start(f32[768]{0:T(1024)} %param.30) | copy-start | bytes 9220
  181.5 96.3 %reduce-scatter.10.cloned.1.call-start = ((), (), s32[]{:S(2)}) async-start(), calls=%async_computation.10 | async-start | bytes 1474560 | tf_op jit(solution)/shard_map/reduce_scatter | solution.py:175
  240.9 6.1 %copy-start.35 = (bf16[768,768]{1,0:T(8,128)(2,1)S(1)}, bf16[768,768]{1,0:T(8,128)(2,1)}, u32[]{:S(2)}) copy-start(bf16[768,768]{1,0:T(8,128)(2,1)} %param.29) | copy-start | bytes 3538948
  249.1 28.7 %copy-start.4 = (bf16[192,768]{1,0:T(8,128)(2,1)S(1)}, bf16[192,768]{1,0:T(8,128)(2,1)}, u32[]{:S(2)}) copy-start(bf16[192,768]{1,0:T(8,128)(2,1)} %reduce-scatter.6.cloned.1.call-done) | copy-start | bytes 884740
  249.1 59.6 %reduce-scatter.8.cloned.1.call-start = ((), (), s32[]{:S(2)}) async-start(), calls=%async_computation.9 | async-start | bytes 1474560 | tf_op jit(solution)/shard_map/reduce_scatter | solution.py:159
  253.5 57.4 %copy-start.6 = (bf16[1,192,768]{2,1,0:T(8,128)(2,1)S(1)}, bf16[1,192,768]{2,1,0:T(8,128)(2,1)}, u32[]{:S(2)}) copy-start(bf16[1,192,768]{2,1,0:T(8,128)(2,1)} %param.35) | copy-start | bytes 884740
  253.5 87.8 %copy-start.11 = (bf16[192,768]{1,0:T(8,128)(2,1)S(1)}, bf16[192,768]{1,0:T(8,128)(2,1)}, u32[]{:S(2)}) copy-start(bf16[192,768]{1,0:T(8,128)(2,1)} %param.25) | copy-start | bytes 884740
  253.5 87.8 %all-gather.15.cloned.1.call-start = ((), (), s32[]{:S(2)}) async-start(), calls=%async_computation.11 | async-start | bytes 1474560 | tf_op jit(solution)/shard_map/all_gather | solution.py:185
  310.8 3.1 copy-start.29
  312.3 129.7 %reduce-scatter.12.cloned.1.call-start = ((), (), s32[]{:S(2)}) async-start(), calls=%async_computation.12 | async-start | bytes 2949120 | tf_op jit(solution)/shard_map/reduce_scatter | solution.py:246
  409.8 33.3 %copy-start.38 = (bf16[3,768,192]{1,2,0:T(8,128)(2,1)S(1)}, bf16[3,768,192]{1,2,0:T(8,128)(2,1)}, u32[]{:S(2)}) copy-start(bf16[3,768,192]{1,2,0:T(8,128)(2,1)} %param.23) | copy-start | bytes 2654212
  409.8 65.0 %reduce-scatter.14.cloned.1.call-start = ((), (), s32[]{:S(2)}) async-start(), calls=%async_computation.13 | async-start | bytes 1474560 | tf_op jit(solution)/shard_map/reduce_scatter | solution.py:267
  445.4 4.4 copy-start.40
  445.4 146.1 %all-reduce.5.cloned.1.call-start = ((), (), s32[]{:S(2)}) async-start(), calls=%async_computation.16 | async-start | bytes 14155776 | tf_op jit(solution)/shard_map/psum | solution.py:278
  445.5 4.3 copy-start.37
  445.5 4.3 copy-start.41
  449.8 2.9 copy-start.5
  449.8 4.1 copy-start.36
  456.0 18.9 %copy-start.14 = (f32[768]{0:T(1024)S(1)}, f32[768]{0:T(1024)}, u32[]{:S(2)}) copy-start(f32[768]{0:T(1024)} %param.21) | copy-start | bytes 9220
  456.0 18.9 %copy-start.17 = (f32[192]{0:T(256)S(1)}, f32[192]{0:T(256)}, u32[]{:S(2)}) copy-start(f32[192]{0:T(256)} %copy-done.16) | copy-start | bytes 2308
  456.0 20.1 %copy-start.27 = (f32[192]{0:T(256)S(1)}, f32[192]{0:T(256)}, u32[]{:S(2)}) copy-start(f32[192]{0:T(256)} %copy-done.26) | copy-start | bytes 2308
  456.0 20.2 %copy-start.20 = (f32[192]{0:T(256)S(1)}, f32[192]{0:T(256)}, u32[]{:S(2)}) copy-start(f32[192]{0:T(256)} %copy-done.19) | copy-start | bytes 2308
  456.0 21.5 %copy-start.21 = (f32[768]{0:T(1024)S(1)}, f32[768]{0:T(1024)}, u32[]{:S(2)}) copy-start(f32[768]{0:T(1024)} %get-tuple-element.276) | copy-start | bytes 9220
  456.0 21.5 %copy-start.22 = (f32[768]{0:T(1024)S(1)}, f32[768]{0:T(1024)}, u32[]{:S(2)}) copy-start(f32[768]{0:T(1024)} %get-tuple-element.280) | copy-start | bytes 9220
  456.0 21.5 %copy-start.23 = (f32[768]{0:T(1024)S(1)}, f32[768]{0:T(1024)}, u32[]{:S(2)}) copy-start(f32[768]{0:T(1024)} %get-tuple-element.349) | copy-start | bytes 9220
  456.0 61.7 %copy-start.30 = (f32[192]{0:T(256)S(1)}, f32[192]{0:T(256)}, u32[]{:S(2)}) copy-start(f32[192]{0:T(256)} %copy-done.29) | copy-start | bytes 2308
  591.5 3.0 copy-start.12
  591.5 3.8 copy-start.8
  595.3 2.5 copy-start.7
  595.3 3.9 copy-start.1
  (10 other events, 10.2 us)
Sparse Core Ops, SparseCore 0:
  12.8 32.9 all-gather.8
  50.4 16.6 all-gather.16
  69.2 17.4 all-gather.10
  147.3 29.3 reduce-scatter.5
  181.1 28.8 all-gather.12
  211.4 29.4 all-gather.18
  249.2 28.5 reduce-scatter.9
  280.7 27.9 reduce-scatter.7
  312.5 28.8 all-gather.14
  410.0 32.0 reduce-scatter.11
  445.5 29.3 reduce-scatter.13
  479.6 111.9 all-reduce.4
where the time goes:
time: 609 us; the launch traced here: 606 us
  waiting for transfers between devices  312 us (51%)
  matrix products  80 us (13%)
  local copies, waits for them, and re-layouts  76.5 us (13%)
  blocking collectives  54.9 us (9%)
  other arithmetic  50.8 us (8%)
  loops' own time  16 us (3%)
  between operations  14.8 us (2%)
    psum x1, waiting for transfers between devices, per_device(): lax.psum((grad_project, grad_project_bias, grad_attend, grad_expand, grad...  71.8 us
    psum x1, blocking collectives, per_device(): lax.psum((grad_first_gain, grad_first_shift, grad_attend_bias, grad_secon...  40.2 us
    all_gather x1, waiting for transfers between devices, per_device(): hidden1_full = lax.all_gather(hidden1, 'tensor', axis=0, tiled=True)  33.1 us
    reduce_scatter x1, waiting for transfers between devices, per_device(): lax.psum_scatter(key_terms.reshape(seq_len, 2 * local_width).astype(jnp.b...  32.1 us
    reduce_scatter x1, waiting for transfers between devices, per_device(): lax.psum_scatter(jnp.dot(part, attend_weight, preferred_element_type=jnp....  29.4 us
    reduce_scatter x1, waiting for transfers between devices, per_device(): lax.psum_scatter(jnp.dot(part, shrink_weight, preferred_element_type=jnp....  28.2 us
    all_gather x1, waiting for transfers between devices, per_device(): hidden2_full = lax.all_gather(hidden2, 'tensor', axis=0, tiled=True)  28.2 us
    all_gather x1, waiting for transfers between devices, per_device(): lax.all_gather(grad_middle_low, 'tensor', axis=0, tiled=True)  27.4 us
  transfers between devices with their start and end apart: 12, of which 11 were waited for; matrix products, arithmetic and copies ran while one was open for 9% of the time, Pallas kernels for 0%

commit v1 on v0

--- a/solution.py
+++ b/solution.py
@@ -6,6 +6,18 @@
 HEAD_DIM = 64
 NEG_FILL = -1e30
 NORM_EPS = 1e-05
+
+
+def gather_by_bits(x, axis, dim):
+    ways, here = (lax.axis_size(axis), lax.axis_index(axis))
+    grown, reach = (x, 1)
+    while reach < ways:
+        theirs = lax.ppermute(grown, axis, [(d, d ^ reach) for d in range(ways)])
+        mine_first = jnp.concatenate([grown, theirs], axis=dim)
+        theirs_first = jnp.concatenate([theirs, grown], axis=dim)
+        grown = jnp.where(here & reach == 0, mine_first, theirs_first)
+        reach = 2 * reach
+    return grown
 
 
 def layer_norm(values):
@@ -164,7 +176,7 @@
     ).astype(jnp.float32)
     outputs = (middle + feed_sum + shrink_bias).astype(jnp.bfloat16)[None]
     grad_out = cotangent[0]
-    grad_full = lax.all_gather(grad_out, "tensor", axis=0, tiled=True)
+    grad_full = gather_by_bits(grad_out, "tensor", 0)
     grad_shrink = cross_rows(activ, grad_full)
     grad_shrink_bias = jnp.sum(grad_out.astype(jnp.float32), axis=0)
     grad_act = jnp.dot(grad_full, shrink_weight.T, preferred_element_type=jnp.float32)

time: 609 us -> 597 us (0.980)
  waiting for transfers between devices: 312 us -> 303 us
    all_gather x1 -> x0, waiting for transfers between devices: 26.8 us -> none  [per_device(): grad_full = lax.all_gather(grad_out, 'tensor', axis=0, tiled=True)]
    all_gather x1, waiting for transfers between devices: 28.2 us -> 39.2 us  [per_device(): hidden2_full = lax.all_gather(hidden2, 'tensor', axis=0, tiled=True)]
    ppermute x0 -> x2, waiting for transfers between devices: none -> 9.7 us  [gather_by_bits(): theirs = lax.ppermute(grown, axis, [(d, d ^ reach) for d in range(ways)])]
    unnamed x89 -> x91, local copies, waits for them, and re-layouts: 13.4 us -> 12.4 us
  transfers between devices with their start and end apart: 12 -> 13, of which waited for: 11 -> 12; matrix products, arithmetic and copies ran while one was open for 9% -> 10% of each run, Pallas kernels for 0% -> 0%
where the time goes in v1:
time: 597 us; the launch traced here: 594 us
  waiting for transfers between devices  303 us (51%)
  matrix products  80.3 us (13%)
  local copies, waits for them, and re-layouts  75.5 us (13%)
  blocking collectives  55.3 us (9%)
  other arithmetic  47.2 us (8%)
  loops' own time  16.2 us (3%)
  between operations  14.5 us (2%)
    psum x1, waiting for transfers between devices, per_device(): lax.psum((grad_project, grad_project_bias, grad_attend, grad_expand, grad...  71.9 us
    psum x1, blocking collectives, per_device(): lax.psum((grad_first_gain, grad_first_shift, grad_attend_bias, grad_secon...  40.3 us
    all_gather x1, waiting for transfers between devices, per_device(): hidden2_full = lax.all_gather(hidden2, 'tensor', axis=0, tiled=True)  39.2 us
    all_gather x1, waiting for transfers between devices, per_device(): hidden1_full = lax.all_gather(hidden1, 'tensor', axis=0, tiled=True)  33.1 us
    reduce_scatter x1, waiting for transfers between devices, per_device(): lax.psum_scatter(key_terms.reshape(seq_len, 2 * local_width).astype(jnp.b...  32 us
    reduce_scatter x1, waiting for transfers between devices, per_device(): lax.psum_scatter(jnp.dot(part, attend_weight, preferred_element_type=jnp....  29.4 us
    reduce_scatter x1, waiting for transfers between devices, per_device(): lax.psum_scatter(jnp.dot(part, shrink_weight, preferred_element_type=jnp....  28.2 us
    all_gather x1, waiting for transfers between devices, per_device(): lax.all_gather(grad_middle_low, 'tensor', axis=0, tiled=True)  27.4 us
  transfers between devices with their start and end apart: 13, of which 12 were waited for; matrix products, arithmetic and copies ran while one was open for 10% of the time, Pallas kernels for 0%

profile of v1, /device:TPU:0, one launch (start us, length us, event | category | flops | bytes accessed | tf_op | source)
XLA Modules:
  0.0 594.1 jit_solution(4764589977020471293)
XLA Ops:
  9.7 1.9 fusion.48
  11.6 33.1 %all-gather.7.cloned.1.call-done = bf16[768,768]{1,0:T(8,128)(2,1)} async-done(((bf16[192,768]{1,0:T(8,128)(2,1)}), bf16[768,768]{1,0:T(8,128)(2,1)}) %all-gather.7.cloned.1.call-update) | async-done | bytes 1179664 | tf_op jit(solution)/shard_map/all_gather | solution.py:106
  44.8 2.4 fusion.85
  49.4 1.9 fusion.56
  51.6 17.4 %gather_fusion = s32[3072]{0:T(1024)S(1)} fusion(s32[3072]{0:T(1024)S(1)} %bitcast.255, s32[3072]{0:T(1024)S(1)} %broadcast_clamp_fusion), kind=kCustom, calls=%fused_computation | custom fusion | bytes 36864 | tf_op jit(solution)/shard_map/jit(_take)/gather | solution.py:100
  73.5 3.5 reshape.298
  78.4 7.2 %all-gather.9.cloned.1.call-done = bf16[3072,192]{0,1:T(8,128)(2,1)} async-done(((bf16[768,192]{0,1:T(8,128)(2,1)}), bf16[3072,192]{0,1:T(8,128)(2,1)}) %all-gather.9.cloned.1.call-update) | async-done | bytes 1179664 | tf_op jit(solution)/shard_map/all_gather | solution.py:151
  85.6 2.4 copy.58
  88.0 50.4 %while.28 = (s32[]{:T(128)}, f32[768,3]{0,1:T(4,128)S(1)}, f32[768,3]{0,1:T(4,128)}, f32[768,3,64]{0,2,1:T(8,128)S(1)}, s32[768]{0:T(1024)}, /*index=5*/s32[4]{0...) while((s32[]{:T(128)}, f32[768,3]{0,1:T(4,128)S(1)}, ...), condition=%wide.region_6.7_spmd.clone, body=%wide.region_3.6_spmd.clone.sunk | while | flops 478211328 | bytes 27083024 | solution.py:70
  96.4 1.8 fusion.146
  98.2 2.3 fusion.148
  109.0 1.8 fusion.146
  110.9 2.3 fusion.148
  121.6 1.8 fusion.146
  123.5 2.3 fusion.148
  134.2 1.8 fusion.146
  136.0 2.3 fusion.148
  139.2 2.5 convolution_convert_fusion.2
  141.8 29.4 %reduce-scatter.6.cloned.1.call-done = bf16[192,768]{1,0:T(8,128)(2,1)} async-done(((bf16[768,768]{1,0:T(8,128)(2,1)}), bf16[192,768]{1,0:T(8,128)(2,1)}) %reduce-scatter.6.cloned.1.call-update) | async-done | bytes 294928 | tf_op jit(solution)/shard_map/reduce_scatter | solution.py:159
  173.6 1.9 add_convert_fusion.2
  175.9 8.3 %collective-permute-done = bf16[192,768]{1,0:T(8,128)(2,1)S(1)} collective-permute-done((bf16[192,768]{1,0:T(8,128)(2,1)S(1)}, bf16[192,768]{1,0:T(8,128)(2,1)S(1)}, u32[]{:S(2)}, u32[]{:S(2)}) %collective-permute-start) | collective-permute-done | bytes 294944 | tf_op jit(solution)/shard_map/ppermute | solution.py:15
  186.6 39.2 %all-gather.11.cloned.1.call-done = bf16[768,768]{1,0:T(8,128)(2,1)} async-done(((bf16[192,768]{1,0:T(8,128)(2,1)}), bf16[768,768]{1,0:T(8,128)(2,1)}) %all-gather.11.cloned.1.call-update) | async-done | bytes 1179664 | tf_op jit(solution)/shard_map/all_gather | solution.py:167
  225.8 2.7 fusion.86
  229.9 4.7 convert_reduce_fusion
  235.7 2.1 convolution_convert_fusion
  237.9 4.3 convolution_convert_fusion.1
  242.3 23.9 %reduce-scatter.10.cloned.1.call-done = bf16[192,768]{1,0:T(8,128)(2,1)} async-done(((bf16[768,768]{1,0:T(8,128)(2,1)}), bf16[192,768]{1,0:T(8,128)(2,1)}) %reduce-scatter.10.cloned.1.call-update) | async-done | bytes 294928 | tf_op jit(solution)/shard_map/reduce_scatter | solution.py:187
  266.2 1.9 fusion.53
  268.8 28.2 %reduce-scatter.8.cloned.1.call-done = bf16[192,768]{1,0:T(8,128)(2,1)} async-done(((bf16[768,768]{1,0:T(8,128)(2,1)}), bf16[192,768]{1,0:T(8,128)(2,1)}) %reduce-scatter.8.cloned.1.call-update) | async-done | bytes 294928 | tf_op jit(solution)/shard_map/reduce_scatter | solution.py:171
  297.0 2.2 fusion.82
  302.3 27.4 %all-gather.13.cloned.1.call-done = bf16[768,768]{1,0:T(8,128)(2,1)} async-done(((bf16[192,768]{1,0:T(8,128)(2,1)}), bf16[768,768]{1,0:T(8,128)(2,1)}) %all-gather.13.cloned.1.call-update) | async-done | bytes 1179664 | tf_op jit(solution)/shard_map/all_gather | solution.py:197
  329.7 1.8 convolution_convert_fusion.3
  332.3 62.4 %while.29 = (s32[]{:T(128)}, f32[768,3,64]{0,2,1:T(8,128)S(1)}, bf16[4,768,384]{1,2,0:T(8,128)(2,1)}, s32[4]{0:T(128)}, bf16[3072,192]{0,1:T(8,128)(2,1)}, /*ind...) while((s32[]{:T(128)}, f32[768,3,64]{0,2,1:T(8,128)S(1)}, ...), condition=%wide.region_16.17_spmd.clone, body=%wide.region_15.16_spmd.clone.sunk | while | flops 1153843200 | bytes 39902472 | solution.py:257
  342.4 2.7 fusion.160
  358.1 2.7 fusion.160
  373.7 2.7 fusion.160
  389.2 2.7 fusion.160
  394.7 3.4 copy.56
  398.2 32.0 %reduce-scatter.12.cloned.1.call-done = bf16[768,384]{0,1:T(8,128)(2,1)} async-done(((bf16[3072,384]{0,1:T(8,128)(2,1)}), bf16[768,384]{0,1:T(8,128)(2,1)}) %reduce-scatter.12.cloned.1.call-update) | async-done | bytes 589840 | tf_op jit(solution)/shard_map/reduce_scatter | solution.py:258
  431.4 2.2 bitcast_convert_fusion
  433.6 4.3 fusion.88
  438.0 4.9 fusion.64
  444.1 2.1 convolution_bitcast_fusion
  447.4 15.0 %all-reduce.1 = (f32[2,192]{1,0:T(2,128)}, f32[768]{0:T(1024)}) all-reduce(f32[2,192]{1,0:T(2,128)S(1)} %pad_maximum_fusion.3, f32[768]{0:T(1024)S(1)} %copy-done.35), channel_id=1, replica_groups=mesh['tensor'=4,'context'=4,'dp'=2] {'context','dp'}, use_global_device_ids=true, to_apply=%region_28.29 | all-reduce | flops 1152 | bytes 9216 | tf_op jit(solution)/shard_map/psum | solution.py:290
  465.7 40.3 %all-reduce = (f32[768]{0:T(1024)}, f32[768]{0:T(1024)}, f32[768]{0:T(1024)}, f32[768]{0:T(1024)}, f32[768]{0:T(1024)}, /*index=5*/f32[768]{0:T(1024)}) all-reduce(f32[768]{0:T(1024)S(1)} %get-tuple-element.278, f32[768]{0:T(1024)S(1)} %get-tuple-element.281, ...), channel_id=1, replica_groups=mesh['tensor'=4,'context'=4,'dp'=2] {'tensor','context','dp'}, use_global_device_ids=true, to_apply=%region_22.23 | all-reduce | flops 4608 | bytes 36864 | tf_op jit(solution)/shard_map/psum | solution.py:294
  506.0 2.0 fusion.62
  508.0 71.9 %all-reduce.5.cloned.1.call-done = (f32[3,768,192]{1,2,0:T(8,128)}, f32[192,768]{1,0:T(8,128)}, f32[768,768]{1,0:T(8,128)}, f32[768,768]{1,0:T(8,128)}) async-done(((f32[3,768,192]{1,2,0:T(8,128)}, f32[192,768]{1,0:T(8,128)}, f32[768,768]{1,0:T(8,128)}, f32[768,768]{1,0:T(8,128)}), (f32[3,768,192]{1,2,0:T(8,128)}, f32[192,768]{1,0:T(8,128)}, f32[768,768]{1,0:T(8,128)}, ...) | async-done | bytes 7077904 | tf_op jit(solution)/shard_map/psum | solution.py:290
  579.9 2.9 copy.85
  (261 shorter events, 105.0 us)
Async XLA Ops:
  7.2 222.7 %copy-start = (bf16[768,768]{1,0:T(8,128)(2,1)S(1)}, bf16[768,768]{1,0:T(8,128)(2,1)}, u32[]{:S(2)}) copy-start(bf16[768,768]{1,0:T(8,128)(2,1)} %param.31) | copy-start | bytes 3538948
  7.2 37.5 %all-gather.7.cloned.1.call-start = ((), (), s32[]{:S(2)}) async-start(), calls=%async_computation.5 | async-start | bytes 1474560 | tf_op jit(solution)/shard_map/all_gather | solution.py:106
  8.4 36.3 %copy-start.18 = (f32[192]{0:T(256)}, f32[192]{0:T(256)S(1)}, u32[]{:S(2)}) copy-start(f32[192]{0:T(256)S(1)} %broadcast_multiply_fusion.2) | copy-start | bytes 2308
  9.6 35.1 %copy-start.29 = (f32[192]{0:T(256)}, f32[192]{0:T(256)S(1)}, u32[]{:S(2)}) copy-start(f32[192]{0:T(256)S(1)} %fusion.50) | copy-start | bytes 2308
  9.6 35.1 %copy-start.21 = (f32[192]{0:T(256)}, f32[192]{0:T(256)S(1)}, u32[]{:S(2)}) copy-start(f32[192]{0:T(256)S(1)} %fusion.75) | copy-start | bytes 2308
  11.6 61.9 %all-gather.15.cloned.1.call-start = ((), (), s32[]{:S(2)}) async-start(), calls=%async_computation.14 | async-start | bytes 1474560 | tf_op jit(solution)/shard_map/all_gather | solution.py:150
  44.8 4.5 copy-start.36
  44.8 6.6 %copy-start.37 = (s32[8]{0:T(128)S(1)}, s32[8]{0:T(128)}, u32[]{:S(2)}) copy-start(s32[8]{0:T(128)} %param.34) | copy-start | bytes 100
  47.2 4.3 copy-start.2
  49.2 36.4 %all-gather.9.cloned.1.call-start = ((), (), s32[]{:S(2)}) async-start(), calls=%async_computation.6 | async-start | bytes 1474560 | tf_op jit(solution)/shard_map/all_gather | solution.py:151
  51.3 119.9 %reduce-scatter.6.cloned.1.call-start = ((), (), s32[]{:S(2)}) async-start(), calls=%async_computation.7 | async-start | bytes 1474560 | tf_op jit(solution)/shard_map/reduce_scatter | solution.py:159
  138.3 32.9 %copy-start.3 = (bf16[1,192,768]{2,1,0:T(8,128)(2,1)S(1)}, bf16[1,192,768]{2,1,0:T(8,128)(2,1)}, u32[]{:S(2)}) copy-start(bf16[1,192,768]{2,1,0:T(8,128)(2,1)} %param.20) | copy-start | bytes 884740
  138.4 32.9 %copy-start.15 = (f32[768]{0:T(1024)S(1)}, f32[768]{0:T(1024)}, u32[]{:S(2)}) copy-start(f32[768]{0:T(1024)} %param.26) | copy-start | bytes 9220
  138.4 35.2 %copy-start.17 = (f32[768]{0:T(1024)S(1)}, f32[768]{0:T(1024)}, u32[]{:S(2)}) copy-start(f32[768]{0:T(1024)} %param.27) | copy-start | bytes 9220
  138.4 35.2 %copy-start.34 = (f32[768]{0:T(1024)S(1)}, f32[768]{0:T(1024)}, u32[]{:S(2)}) copy-start(f32[768]{0:T(1024)} %param.28) | copy-start | bytes 9220
  139.2 36.6 %copy-start.6 = (bf16[1,192,768]{2,1,0:T(8,128)(2,1)S(1)}, bf16[1,192,768]{2,1,0:T(8,128)(2,1)}, u32[]{:S(2)}) copy-start(bf16[1,192,768]{2,1,0:T(8,128)(2,1)} %param.35) | copy-start | bytes 884740
  141.8 84.0 %all-gather.11.cloned.1.call-start = ((), (), s32[]{:S(2)}) async-start(), calls=%async_computation.8 | async-start | bytes 1474560 | tf_op jit(solution)/shard_map/all_gather | solution.py:167
  172.4 3.4 copy-start.20
  175.5 90.6 %reduce-scatter.10.cloned.1.call-start = ((), (), s32[]{:S(2)}) async-start(), calls=%async_computation.10 | async-start | bytes 1474560 | tf_op jit(solution)/shard_map/reduce_scatter | solution.py:187
  175.8 8.4 %collective-permute-start = (bf16[192,768]{1,0:T(8,128)(2,1)S(1)}, bf16[192,768]{1,0:T(8,128)(2,1)S(1)}, u32[]{:S(2)}, u32[]{:S(2)}) collective-permute-start(bf16[192,768]{1,0:T(8,128)(2,1)S(1)} %bitcast.269), channel_id=1, source_target_pairs={{0,8},{8,0},{16,24},{24,16},{1,9},{9,1},{17,25},{25,17},{2,10},{10... | collective-permute-start | bytes 884744 | tf_op jit(solution)/shard_map/ppermute | solution.py:15
  185.2 44.7 %collective-permute-start.1 = (bf16[384,768]{1,0:T(8,128)(2,1)}, bf16[384,768]{1,0:T(8,128)(2,1)}, u32[]{:S(2)}, u32[]{:S(2)}) collective-permute-start(bf16[384,768]{1,0:T(8,128)(2,1)} %maximum_select_fusion.1), channel_id=1, source_target_pairs={{0,16},{8,24},{16,0},{24,8},{1,17},{9,25},{17,1},{25,9},{2,18},{10... | collective-permute-start | bytes 1769480 | tf_op jit(solution)/shard_map/ppermute | solution.py:15
  186.6 43.3 %copy-start.41 = (f32[768]{0:T(1024)S(1)}, f32[768]{0:T(1024)}, u32[]{:S(2)}) copy-start(f32[768]{0:T(1024)} %param.30) | copy-start | bytes 9220
  228.5 6.1 %copy-start.43 = (f32[768,768]{1,0:T(8,128)}, f32[768,768]{1,0:T(8,128)S(1)}, u32[]{:S(2)}) copy-start(f32[768,768]{1,0:T(8,128)S(1)} %fusion.86) | copy-start | bytes 7077892
  228.5 7.1 %copy-start.38 = (bf16[768,768]{1,0:T(8,128)(2,1)S(1)}, bf16[768,768]{1,0:T(8,128)(2,1)}, u32[]{:S(2)}) copy-start(bf16[768,768]{1,0:T(8,128)(2,1)} %param.29) | copy-start | bytes 3538948
  237.8 28.3 %copy-start.4 = (bf16[192,768]{1,0:T(8,128)(2,1)S(1)}, bf16[192,768]{1,0:T(8,128)(2,1)}, u32[]{:S(2)}) copy-start(bf16[192,768]{1,0:T(8,128)(2,1)} %reduce-scatter.6.cloned.1.call-done) | copy-start | bytes 884740
  237.8 59.2 %reduce-scatter.8.cloned.1.call-start = ((), (), s32[]{:S(2)}) async-start(), calls=%async_computation.9 | async-start | bytes 1474560 | tf_op jit(solution)/shard_map/reduce_scatter | solution.py:171
  242.2 87.5 %copy-start.11 = (bf16[192,768]{1,0:T(8,128)(2,1)S(1)}, bf16[192,768]{1,0:T(8,128)(2,1)}, u32[]{:S(2)}) copy-start(bf16[192,768]{1,0:T(8,128)(2,1)} %param.25) | copy-start | bytes 884740
  242.2 87.4 %all-gather.13.cloned.1.call-start = ((), (), s32[]{:S(2)}) async-start(), calls=%async_computation.11 | async-start | bytes 1474560 | tf_op jit(solution)/shard_map/all_gather | solution.py:197
  300.7 129.6 %reduce-scatter.12.cloned.1.call-start = ((), (), s32[]{:S(2)}) async-start(), calls=%async_computation.12 | async-start | bytes 2949120 | tf_op jit(solution)/shard_map/reduce_scatter | solution.py:258
  398.1 33.2 %copy-start.40 = (bf16[3,768,192]{1,2,0:T(8,128)(2,1)S(1)}, bf16[3,768,192]{1,2,0:T(8,128)(2,1)}, u32[]{:S(2)}) copy-start(bf16[3,768,192]{1,2,0:T(8,128)(2,1)} %param.23) | copy-start | bytes 2654212
  398.1 64.9 %reduce-scatter.14.cloned.1.call-start = ((), (), s32[]{:S(2)}) async-start(), calls=%async_computation.13 | async-start | bytes 1474560 | tf_op jit(solution)/shard_map/reduce_scatter | solution.py:279
  433.6 4.4 copy-start.42
  433.6 146.3 %all-reduce.5.cloned.1.call-start = ((), (), s32[]{:S(2)}) async-start(), calls=%async_computation.15 | async-start | bytes 14155776 | tf_op jit(solution)/shard_map/psum | solution.py:290
  433.6 4.3 copy-start.44
  438.0 4.9 copy-start.5
  438.0 6.1 %copy-start.39 = (bf16[768,768]{1,0:T(8,128)(2,1)S(1)}, bf16[768,768]{1,0:T(8,128)(2,1)}, u32[]{:S(2)}) copy-start(bf16[768,768]{1,0:T(8,128)(2,1)} %all-gather.7.cloned.1.call-done) | copy-start | bytes 3538948
  446.2 16.9 %copy-start.16 = (f32[768]{0:T(1024)S(1)}, f32[768]{0:T(1024)}, u32[]{:S(2)}) copy-start(f32[768]{0:T(1024)} %param.21) | copy-start | bytes 9220
  446.2 16.9 %copy-start.19 = (f32[192]{0:T(256)S(1)}, f32[192]{0:T(256)}, u32[]{:S(2)}) copy-start(f32[192]{0:T(256)} %copy-done.18) | copy-start | bytes 2308
  446.2 18.1 %copy-start.30 = (f32[192]{0:T(256)S(1)}, f32[192]{0:T(256)}, u32[]{:S(2)}) copy-start(f32[192]{0:T(256)} %copy-done.29) | copy-start | bytes 2308
  446.2 18.1 %copy-start.22 = (f32[192]{0:T(256)S(1)}, f32[192]{0:T(256)}, u32[]{:S(2)}) copy-start(f32[192]{0:T(256)} %copy-done.21) | copy-start | bytes 2308
  446.2 19.5 %copy-start.23 = (f32[768]{0:T(1024)S(1)}, f32[768]{0:T(1024)}, u32[]{:S(2)}) copy-start(f32[768]{0:T(1024)} %get-tuple-element.276) | copy-start | bytes 9220
  446.2 19.5 %copy-start.24 = (f32[768]{0:T(1024)S(1)}, f32[768]{0:T(1024)}, u32[]{:S(2)}) copy-start(f32[768]{0:T(1024)} %get-tuple-element.280) | copy-start | bytes 9220
  446.2 19.5 %copy-start.25 = (f32[768]{0:T(1024)S(1)}, f32[768]{0:T(1024)}, u32[]{:S(2)}) copy-start(f32[768]{0:T(1024)} %get-tuple-element.349) | copy-start | bytes 9220
  446.2 19.5 %copy-start.26 = (f32[768]{0:T(1024)S(1)}, f32[768]{0:T(1024)}, u32[]{:S(2)}) copy-start(f32[768]{0:T(1024)} %get-tuple-element.362) | copy-start | bytes 9220
  446.3 59.8 %copy-start.33 = (f32[192]{0:T(256)S(1)}, f32[192]{0:T(256)}, u32[]{:S(2)}) copy-start(f32[192]{0:T(256)} %copy-done.32) | copy-start | bytes 2308
  579.9 3.0 copy-start.14
  579.9 3.8 copy-start.8
  583.7 3.9 copy-start.1
  (20 other events, 34.1 us)
Sparse Core Ops, SparseCore 0:
  11.7 32.9 all-gather.6
  49.3 16.6 all-gather.14
  68.1 17.4 all-gather.8
  141.9 29.3 reduce-scatter.5
  175.6 50.1 all-gather.10
  237.9 28.1 reduce-scatter.9
  269.0 27.9 reduce-scatter.7
  300.8 28.8 all-gather.12
  398.3 31.9 reduce-scatter.11
  433.7 29.3 reduce-scatter.13
  467.9 111.9 all-reduce.4
